TPU v7x, 512 devices: a whole 4x4x16 slice. The times are simulated.
512 devices in a mesh: row: 32 (over z, core), col: 16 (over x, y).
Axes of the slice: x: 4, y: 4, z: 16, core: 2. Of those that a mesh axis runs over, the one named last changes fastest.
Arguments:
- front_entries: float32 [16384, 16384], P('row', 'col'), may hold values from 0 to 3, as said below
- tile_group: int32 [32], replicated, may hold values from 0 to 3
- child_factor: bfloat16 [16384, 256], P('row', 'col'), may hold values from -0.375 to 0.375
- row_map: int32 [128], replicated, may hold values from 0 to 127, as said below
Outputs:
- factor_panels: bfloat16 [16384, 512], P('row', 'col')
- schur_block: float32 [16384, 16384], P('row', 'col')
Inputs may be any that keep to these rules, and one draw needn't show every extreme that they name: `front_entries`: Symmetric; assembled is positive definite. `row_map`: A permutation of the parent tiles. The tile in row block r (blocks of 512 rows) goes to a parent tile in row block r or in the row block whose index differs from r in the highest bit.
All inputs are finite; a program needn't handle non-finite values.
Results may differ from a plain program's by a relative error of at most 0.0026.
Values may be sent and summed in bfloat16 or wider, within the bound.
A program may use at most 64 MiB of HBM per device.

v0:
```python
import jax
import jax.numpy as jnp
from jax import lax
from jax.sharding import PartitionSpec as P

PW = 256
NP = 2
TS = 128
MT = 512


def swapped(value, axis, stride):
    mask = 2**stride
    pairs = [(source, source ^ mask) for source in range(lax.axis_size(axis))]
    return lax.ppermute(value, axis, pairs)


def broadcast(value, axis, source):
    kept = jnp.where(lax.axis_index(axis) == source, value, 0).astype(value.dtype)
    return lax.psum(kept, axis)


def panel_columns(matrix, offset, width_cols, fan_ratio, block_rows):
    return jnp.concatenate(
        [
            matrix[:, q * block_rows + offset : q * block_rows + offset + width_cols]
            for q in range(fan_ratio)
        ],
        axis=1,
    )


def outer_rows(left, right):
    return jnp.einsum("ik,jk->ij", left, right, preferred_element_type=jnp.float32)


def subtract_block(matrix, lead_rows, owner, low, col_from, col_to, base_col):
    region = matrix[low:, base_col + col_from : base_col + col_to]
    return matrix.at[low:, base_col + col_from : base_col + col_to].set(
        region - outer_rows(lead_rows, owner[col_from:col_to])
    )


def right_solve(lower_factor, strip):
    return lax.linalg.triangular_solve(
        lower_factor, strip, left_side=False, lower=True, transpose_a=True
    )


def local(front_entries, tile_group, child_factor, row_map):
    row_count = lax.axis_size("row")
    col_count = lax.axis_size("col")
    fan_ratio = row_count // col_count
    local_rows = front_entries.shape[0]
    local_cols = front_entries.shape[1]
    my_row = lax.axis_index("row")
    my_col = lax.axis_index("col")
    row_tiles = local_rows // MT
    col_tiles = local_cols // MT
    group_rows = lax.dynamic_slice_in_dim(tile_group, my_row * row_tiles, row_tiles)
    group_cols = lax.dynamic_slice_in_dim(tile_group, my_col * col_tiles, col_tiles)
    same_group = (group_rows[:, None] == group_cols[None, :]).astype(jnp.float32)
    masked = (
        front_entries.reshape(row_tiles, MT, col_tiles, MT) * same_group[:, None, :, None]
    ).reshape(local_rows, local_cols)
    child_full = lax.all_gather(child_factor, "col", axis=1, tiled=True)
    child_width = child_full.shape[1]
    partner_full = swapped(child_full, "row", row_count.bit_length() - 2)
    tile_count = local_rows // TS
    partner_row = jnp.bitwise_xor(my_row, row_count // 2)
    own_map = lax.dynamic_slice_in_dim(row_map, my_row * tile_count, tile_count)
    partner_map = lax.dynamic_slice_in_dim(row_map, partner_row * tile_count, tile_count)
    slot_ids = my_row * tile_count + jnp.arange(tile_count, dtype=jnp.int32)

    def place_tiles(tile_map, source):
        chooser = (tile_map[None, :] == slot_ids[:, None]).astype(jnp.bfloat16)
        placed = jnp.dot(
            chooser,
            source.reshape(tile_count, TS * child_width),
            preferred_element_type=jnp.float32,
        )
        return placed.astype(jnp.bfloat16).reshape(local_rows, child_width)

    own_parent = place_tiles(own_map, child_full)
    partner_parent = place_tiles(partner_map, partner_full)
    lower_half = my_row < row_count // 2
    child_wide = jnp.where(
        lower_half,
        jnp.concatenate([own_parent, partner_parent], axis=1),
        jnp.concatenate([partner_parent, own_parent], axis=1),
    )
    child_owners = [broadcast(child_wide, "row", fan_ratio * my_col + q) for q in range(fan_ratio)]
    matrix = jnp.concatenate(
        [
            masked[:, q * local_rows : (q + 1) * local_rows]
            + outer_rows(child_wide, child_owners[q])
            for q in range(fan_ratio)
        ],
        axis=1,
    )
    row_share = PW // row_count
    col_share = PW // col_count
    local_ids = jnp.arange(local_rows)
    coming = None
    outputs = []
    for k in range(NP):
        offset = k * row_share
        panel_strip = panel_columns(matrix, offset, row_share, fan_ratio, local_rows)
        corner = panel_strip[offset : offset + row_share]
        gathered = lax.all_gather(corner, ("row", "col"), axis=0, tiled=True)
        diagonal = (
            gathered.reshape(row_count, col_count, row_share, col_share)
            .transpose(0, 2, 1, 3)
            .reshape(PW, PW)
        )
        lower_factor = jnp.linalg.cholesky(diagonal)
        whole_strip = lax.all_gather(panel_strip, "col", axis=1, tiled=True)
        rounded = right_solve(lower_factor, whole_strip).astype(jnp.bfloat16)
        own_lower = lax.dynamic_slice_in_dim(lower_factor, my_row * row_share, row_share).astype(
            jnp.bfloat16
        )
        rounded = jnp.where((local_ids < offset)[:, None], jnp.zeros_like(rounded), rounded)
        rounded = rounded.at[offset : offset + row_share].set(own_lower)
        outputs.append(lax.dynamic_slice_in_dim(rounded, my_col * col_share, col_share, 1))
        owners = [broadcast(rounded, "row", fan_ratio * my_col + q) for q in range(fan_ratio)]
        low = offset + row_share
        lead_rows = rounded[low:]
        for q in range(fan_ratio):
            matrix = subtract_block(
                matrix, lead_rows, owners[q], low, low, local_rows, q * local_rows
            )
    pivot_done = NP * row_share
    row_keep = local_ids >= pivot_done
    col_keep = jnp.arange(local_cols) % local_rows >= pivot_done
    schur_block = jnp.where(row_keep[:, None] & col_keep[None, :], matrix, jnp.zeros_like(matrix))
    factor_panels = jnp.concatenate(outputs, axis=1)
    return (factor_panels, schur_block)


def solution(mesh):
    placed = (P("row", "col"), P(), P("row", "col"), P())
    return jax.shard_map(
        local,
        mesh=mesh,
        in_specs=placed,
        out_specs=(P("row", "col"), P("row", "col")),
        check_vma=False,
    )
```

profile of v0, /device:TPU:1, one launch (start us, length us, event | category | flops | bytes accessed | tf_op | source)
XLA Modules:
  0.0 1302.7 jit_solution(17513636110733798873)
XLA Ops:
  7.2 19.7 %all_gather.15 = bf16[512,256]{0,1:T(8,128)(2,1)S(1)} all-gather(bf16[512,16]{0,1:T(8,128)(2,1)} %param.21), channel_id=1, replica_groups=mesh['row'=32,'col'=16] {'col'}, dimensions={1}, use_global_device_ids=true | all-gather | bytes 278528 | tf_op jit(solution)/shard_map/all_gather | solution.py:66
  26.9 15.4 %collective-permute-start = (bf16[512,256]{0,1:T(8,128)(2,1)S(1)}, bf16[512,256]{0,1:T(8,128)(2,1)S(1)}, u32[]{:S(2)}, u32[]{:S(2)}) collective-permute-start(bf16[512,256]{0,1:T(8,128)(2,1)S(1)} %all_gather.15), channel_id=1, source_target_pairs={{0,256},{16,272},{32,288},{48,304},{64,320},{80,336},{96,352},{112... | collective-permute-start | bytes 786440 | tf_op jit(solution)/shard_map/ppermute | solution.py:15
  45.5 1.9 copy.30
  51.2 226.5 %all-reduce.12.cloned.1.call-done = (bf16[512,512]{1,0:T(8,128)(2,1)}, bf16[512,512]{1,0:T(8,128)(2,1)}) async-done(((bf16[512,512]{1,0:T(8,128)(2,1)}, bf16[512,512]{1,0:T(8,128)(2,1)}), (bf16[512,512]{1,0:T(8,128)(2,1)}, bf16[512,512]{1,0:T(8,128)(2,1)})) %all-reduce.12.cloned.1.call-update) | async-done | bytes 1048592 | tf_op jit(solution)/shard_map/psum | solution.py:20
  277.7 2.1 convolution_add_fusion.1
  281.4 198.2 %all_gather.16 = f32[4096,16]{1,0:T(8,128)S(1)} all-gather(f32[8,16]{1,0:T(8,128)S(1)} %copy.33), channel_id=1, replica_groups=mesh['row'=32,'col'=16] {'row','col'}, dimensions={0}, use_global_device_ids=true | all-gather | bytes 262656 | tf_op jit(solution)/shard_map/all_gather | solution.py:110
  481.1 11.7 cholesky.130
  492.8 9.8 custom-call.13
  503.1 11.9 cholesky.147
  517.6 3.8 while.10
  521.5 19.7 %custom-call.14 = f32[2,128,128]{1,2,0:T(8,128)S(1)} custom-call(f32[2,128,128]{2,1,0:T(8,128)S(1)} %get-tuple-element.90), custom_call_target="InvertDiagBlocksLowerTriangular" | custom-call | tf_op jit(solution)/shard_map/triangular_solve/custom-call.0 | solution.py:45
  541.2 16.2 %all_gather.17 = f32[512,256]{0,1:T(8,128)S(1)} all-gather(f32[512,16]{0,1:T(8,128)S(1)} %pad_maximum_fusion.1), channel_id=1, replica_groups=mesh['row'=32,'col'=16] {'col'}, dimensions={1}, use_global_device_ids=true | all-gather | bytes 557056 | tf_op jit(solution)/shard_map/all_gather | solution.py:117
  561.5 209.2 %all-reduce.10.cloned.1.call-done = (bf16[512,256]{0,1:T(8,128)(2,1)}, bf16[512,256]{0,1:T(8,128)(2,1)}) async-done(((bf16[512,256]{0,1:T(8,128)(2,1)}, bf16[512,256]{0,1:T(8,128)(2,1)}), (bf16[512,256]{0,1:T(8,128)(2,1)}, bf16[512,256]{0,1:T(8,128)(2,1)})) %all-reduce.10.cloned.1.call-update) | async-done | bytes 524304 | tf_op jit(solution)/shard_map/psum | solution.py:20
  770.6 2.6 convolution_subtract_fusion.1
  773.2 5.4 scatter.21
  780.2 3.4 scatter.24
  783.8 197.6 %all_gather.18 = f32[4096,16]{1,0:T(8,128)S(1)} all-gather(f32[8,16]{1,0:T(8,128)S(1)} %copy.38), channel_id=1, replica_groups=mesh['row'=32,'col'=16] {'row','col'}, dimensions={0}, use_global_device_ids=true | all-gather | bytes 262656 | tf_op jit(solution)/shard_map/all_gather | solution.py:110
  981.5 1.7 copy.39
  983.2 2.6 reshape.257
  986.0 11.7 cholesky.164
  997.8 9.8 custom-call.15
  1008.1 11.7 cholesky.181
  1022.4 4.0 while.11
  1026.5 19.9 %custom-call.16 = f32[2,128,128]{1,2,0:T(8,128)S(1)} custom-call(f32[2,128,128]{2,1,0:T(8,128)S(1)} %get-tuple-element.91), custom_call_target="InvertDiagBlocksLowerTriangular" | custom-call | tf_op jit(solution)/shard_map/triangular_solve/custom-call.0 | solution.py:45
  1046.4 16.3 %all_gather.19 = f32[512,256]{0,1:T(8,128)S(1)} all-gather(f32[512,16]{0,1:T(8,128)S(1)} %pad_maximum_fusion.2), channel_id=1, replica_groups=mesh['row'=32,'col'=16] {'col'}, dimensions={1}, use_global_device_ids=true | all-gather | bytes 557056 | tf_op jit(solution)/shard_map/all_gather | solution.py:117
  1066.2 210.0 %all-reduce.8.cloned.1.call-done = (bf16[512,256]{0,1:T(8,128)(2,1)}, bf16[512,256]{0,1:T(8,128)(2,1)}) async-done(((bf16[512,256]{0,1:T(8,128)(2,1)}, bf16[512,256]{0,1:T(8,128)(2,1)}), (bf16[512,256]{0,1:T(8,128)(2,1)}, bf16[512,256]{0,1:T(8,128)(2,1)})) %all-reduce.8.cloned.1.call-update) | async-done | bytes 524304 | tf_op jit(solution)/shard_map/psum | solution.py:20
  1276.2 2.6 convolution_subtract_fusion.3
  1278.8 5.4 scatter.26
  1284.2 1.6 convolution_subtract_fusion.2
  1285.8 5.6 scatter.29
  1291.4 1.6 and_select_fusion
  1293.0 2.9 copy.45
  (110 shorter events, 30.8 us)
Async XLA Ops:
  7.2 36.9 %copy-start.5 = (s32[32]{0:T(128)S(1)}, s32[32]{0:T(128)}, u32[]{:S(2)}) copy-start(s32[32]{0:T(128)} %param.20) | copy-start | bytes 388
  7.2 270.5 %all-reduce.12.cloned.1.call-start = ((), (), s32[]{:S(2)}) async-start(), calls=%async_computation.2 | async-start | bytes 2097152 | tf_op jit(solution)/shard_map/psum | solution.py:20
  26.9 20.5 %collective-permute-start = (bf16[512,256]{0,1:T(8,128)(2,1)S(1)}, bf16[512,256]{0,1:T(8,128)(2,1)S(1)}, u32[]{:S(2)}, u32[]{:S(2)}) collective-permute-start(bf16[512,256]{0,1:T(8,128)(2,1)S(1)} %all_gather.15), channel_id=1, source_target_pairs={{0,256},{16,272},{32,288},{48,304},{64,320},{80,336},{96,352},{112... | collective-permute-start | bytes 786440 | tf_op jit(solution)/shard_map/ppermute | solution.py:15
  48.3 2.9 copy-start.2
  49.6 721.1 %all-reduce.10.cloned.1.call-start = ((), (), s32[]{:S(2)}) async-start(), calls=%async_computation.1 | async-start | bytes 1048576 | tf_op jit(solution)/shard_map/psum | solution.py:20
  51.2 228.6 %copy-start = (f32[512,1024]{0,1:T(8,128)S(1)}, f32[512,1024]{0,1:T(8,128)}, u32[]{:S(2)}) copy-start(f32[512,1024]{0,1:T(8,128)} %broadcast_multiply_fusion) | copy-start | bytes 6291460
  277.7 2.1 copy-start.3
  277.7 2.1 copy-start.6
  280.3 1.0 copy-start.1
  560.0 716.2 %all-reduce.8.cloned.1.call-start = ((), (), s32[]{:S(2)}) async-start(), calls=%async_computation | async-start | bytes 1048576 | tf_op jit(solution)/shard_map/psum | solution.py:20
  1276.2 8.0 copy-start.4
Sparse Core Ops, SparseCore 0:
  49.7 227.9 all-reduce.11
  560.1 210.4 all-reduce.9
  1065.7 210.4 all-reduce.7
where the time goes:
time: 1310 us; the launch traced here: 1300 us
  waiting for transfers between devices  646 us (49%)
  blocking collectives  448 us (34%)
  other arithmetic  119 us (9%)
  local copies, waits for them, and re-layouts  42.4 us (3%)
  between operations  17.1 us (1%)
  starting transfers between devices  15.5 us (1%)
  matrix products  15 us (1%)
    psum x3, waiting for transfers between devices, broadcast(): return lax.psum(kept, axis)  646 us
    all_gather x2, blocking collectives, local(): gathered = lax.all_gather(corner, ('row', 'col'), axis=0, tiled=True)  396 us
    another operation x14, other arithmetic, local(): lower_factor = jnp.linalg.cholesky(diagonal)  69.3 us
    another operation x5, other arithmetic, right_solve(): lax.linalg.triangular_solve(lower_factor, strip, left_side=False, lower=T...  39.7 us
    all_gather x2, blocking collectives, local(): whole_strip = lax.all_gather(panel_strip, 'col', axis=1, tiled=True)  32.5 us
  transfers between devices with their start and end apart: 4, of which 3 were waited for; matrix products, arithmetic and copies ran while one was open for 1% of the time, Pallas kernels for 0%

commit v1 on v0

--- a/solution.py
+++ b/solution.py
@@ -114,7 +114,9 @@
             .reshape(PW, PW)
         )
         lower_factor = jnp.linalg.cholesky(diagonal)
-        whole_strip = lax.all_gather(panel_strip, "col", axis=1, tiled=True)
+        whole_strip = jnp.concatenate(
+            lax.all_to_all(jnp.stack([panel_strip] * lax.axis_size("col")), "col", 0, 0), axis=1
+        )
         rounded = right_solve(lower_factor, whole_strip).astype(jnp.bfloat16)
         own_lower = lax.dynamic_slice_in_dim(lower_factor, my_row * row_share, row_share).astype(
             jnp.bfloat16

time: 1310 us -> 1280 us (0.977)
  blocking collectives: 448 us -> 416 us
    all_gather x2 -> x0, blocking collectives: 32.5 us -> none  [local(): whole_strip = lax.all_gather(panel_strip, 'col', axis=1, tiled=True)]
  transfers between devices with their start and end apart: 4 -> 6, of which waited for: 3 -> 3; matrix products, arithmetic and copies ran while one was open for 1% -> 4% of each run, Pallas kernels for 0% -> 0%
where the time goes in v1:
time: 1280 us
  waiting for transfers between devices  641 us (50%)
  blocking collectives  416 us (32%)
  other arithmetic  119 us (9%)
  local copies, waits for them, and re-layouts  46.1 us (4%)
  starting transfers between devices  22.7 us (2%)
  between operations  17.2 us (1%)
  matrix products  17.1 us (1%)
    psum x3, waiting for transfers between devices, broadcast(): return lax.psum(kept, axis)  641 us
    all_gather x2, blocking collectives, local(): gathered = lax.all_gather(corner, ('row', 'col'), axis=0, tiled=True)  396 us
    another operation x14, other arithmetic, local(): lower_factor = jnp.linalg.cholesky(diagonal)  69.4 us
    another operation x5, other arithmetic, right_solve(): lax.linalg.triangular_solve(lower_factor, strip, left_side=False, lower=T...  40 us
  transfers between devices with their start and end apart: 6, of which 3 were waited for; matrix products, arithmetic and copies ran while one was open for 4% of the time, Pallas kernels for 0%

profile of v1, /device:TPU:1, one launch (start us, length us, event | category | flops | bytes accessed | tf_op | source)
XLA Modules:
  0.0 1278.8 jit_solution(12751334755396384129)
XLA Ops:
  7.2 19.7 %all_gather.9 = bf16[512,256]{0,1:T(8,128)(2,1)S(1)} all-gather(bf16[512,16]{0,1:T(8,128)(2,1)} %param.21), channel_id=1, replica_groups=mesh['row'=32,'col'=16] {'col'}, dimensions={1}, use_global_device_ids=true | all-gather | bytes 278528 | tf_op jit(solution)/shard_map/all_gather | solution.py:66
  26.9 15.4 %collective-permute-start = (bf16[512,256]{0,1:T(8,128)(2,1)S(1)}, bf16[512,256]{0,1:T(8,128)(2,1)S(1)}, u32[]{:S(2)}, u32[]{:S(2)}) collective-permute-start(bf16[512,256]{0,1:T(8,128)(2,1)S(1)} %all_gather.9), channel_id=1, source_target_pairs={{0,256},{16,272},{32,288},{48,304},{64,320},{80,336},{96,352},{112... | collective-permute-start | bytes 786440 | tf_op jit(solution)/shard_map/ppermute | solution.py:15
  45.5 1.9 copy.32
  51.1 226.5 %all-reduce.12.cloned.1.call-done = (bf16[512,512]{1,0:T(8,128)(2,1)}, bf16[512,512]{1,0:T(8,128)(2,1)}) async-done(((bf16[512,512]{1,0:T(8,128)(2,1)}, bf16[512,512]{1,0:T(8,128)(2,1)}), (bf16[512,512]{1,0:T(8,128)(2,1)}, bf16[512,512]{1,0:T(8,128)(2,1)})) %all-reduce.12.cloned.1.call-update) | async-done | bytes 1048592 | tf_op jit(solution)/shard_map/psum | solution.py:20
  277.6 2.1 convolution_add_fusion.1
  281.3 198.2 %all_gather.10 = f32[4096,16]{1,0:T(8,128)S(1)} all-gather(f32[8,16]{1,0:T(8,128)S(1)} %copy.35), channel_id=1, replica_groups=mesh['row'=32,'col'=16] {'row','col'}, dimensions={0}, use_global_device_ids=true | all-gather | bytes 262656 | tf_op jit(solution)/shard_map/all_gather | solution.py:110
  481.0 11.7 cholesky.130
  492.8 9.8 custom-call.13
  503.1 11.9 cholesky.147
  517.2 3.6 all-to-all-start
  522.2 4.0 while.10
  526.2 19.7 %custom-call.14 = f32[2,128,128]{1,2,0:T(8,128)S(1)} custom-call(f32[2,128,128]{2,1,0:T(8,128)S(1)} %get-tuple-element.90), custom_call_target="InvertDiagBlocksLowerTriangular" | custom-call | tf_op jit(solution)/shard_map/triangular_solve/custom-call.0 | solution.py:45
  550.2 206.8 %all-reduce.10.cloned.1.call-done = (bf16[512,256]{0,1:T(8,128)(2,1)}, bf16[512,256]{0,1:T(8,128)(2,1)}) async-done(((bf16[512,256]{0,1:T(8,128)(2,1)}, bf16[512,256]{0,1:T(8,128)(2,1)}), (bf16[512,256]{0,1:T(8,128)(2,1)}, bf16[512,256]{0,1:T(8,128)(2,1)})) %all-reduce.10.cloned.1.call-update) | async-done | bytes 524304 | tf_op jit(solution)/shard_map/psum | solution.py:20
  757.1 2.6 convolution_subtract_fusion.1
  759.6 5.4 scatter.21
  766.7 3.4 scatter.24
  770.2 197.6 %all_gather.11 = f32[4096,16]{1,0:T(8,128)S(1)} all-gather(f32[8,16]{1,0:T(8,128)S(1)} %copy.40), channel_id=1, replica_groups=mesh['row'=32,'col'=16] {'row','col'}, dimensions={0}, use_global_device_ids=true | all-gather | bytes 262656 | tf_op jit(solution)/shard_map/all_gather | solution.py:110
  967.9 1.7 copy.41
  969.6 2.6 reshape.275
  972.4 11.7 cholesky.164
  984.2 9.8 custom-call.15
  994.5 11.7 cholesky.181
  1008.4 3.6 all-to-all-start.1
  1013.4 4.2 while.11
  1017.6 20.3 %custom-call.16 = f32[2,128,128]{1,2,0:T(8,128)} custom-call(f32[2,128,128]{2,1,0:T(8,128)S(1)} %get-tuple-element.91), custom_call_target="InvertDiagBlocksLowerTriangular" | custom-call | tf_op jit(solution)/shard_map/triangular_solve/custom-call.0 | solution.py:45
  1045.1 207.2 %all-reduce.8.cloned.1.call-done = (bf16[512,256]{0,1:T(8,128)(2,1)}, bf16[512,256]{0,1:T(8,128)(2,1)}) async-done(((bf16[512,256]{0,1:T(8,128)(2,1)}, bf16[512,256]{0,1:T(8,128)(2,1)}), (bf16[512,256]{0,1:T(8,128)(2,1)}, bf16[512,256]{0,1:T(8,128)(2,1)})) %all-reduce.8.cloned.1.call-update) | async-done | bytes 524304 | tf_op jit(solution)/shard_map/psum | solution.py:20
  1252.3 2.6 convolution_subtract_fusion.3
  1254.9 5.4 scatter.26
  1260.4 1.6 convolution_subtract_fusion.2
  1262.0 5.6 scatter.29
  1267.5 1.6 and_select_fusion
  1269.1 2.9 copy.47
  (118 shorter events, 36.6 us)
Async XLA Ops:
  7.2 36.9 %copy-start.5 = (s32[32]{0:T(128)S(1)}, s32[32]{0:T(128)}, u32[]{:S(2)}) copy-start(s32[32]{0:T(128)} %param.20) | copy-start | bytes 388
  7.2 270.5 %all-reduce.12.cloned.1.call-start = ((), (), s32[]{:S(2)}) async-start(), calls=%async_computation.4 | async-start | bytes 2097152 | tf_op jit(solution)/shard_map/psum | solution.py:20
  26.9 20.5 %collective-permute-start = (bf16[512,256]{0,1:T(8,128)(2,1)S(1)}, bf16[512,256]{0,1:T(8,128)(2,1)S(1)}, u32[]{:S(2)}, u32[]{:S(2)}) collective-permute-start(bf16[512,256]{0,1:T(8,128)(2,1)S(1)} %all_gather.9), channel_id=1, source_target_pairs={{0,256},{16,272},{32,288},{48,304},{64,320},{80,336},{96,352},{112... | collective-permute-start | bytes 786440 | tf_op jit(solution)/shard_map/ppermute | solution.py:15
  48.3 2.8 copy-start.2
  51.1 228.7 %copy-start = (f32[512,1024]{0,1:T(8,128)S(1)}, f32[512,1024]{0,1:T(8,128)}, u32[]{:S(2)}) copy-start(f32[512,1024]{0,1:T(8,128)} %broadcast_multiply_fusion) | copy-start | bytes 6291460
  277.6 2.1 copy-start.3
  277.6 2.1 copy-start.6
  280.3 1.0 copy-start.1
  517.2 28.8 %all-to-all-start = ((f32[16,512,16]{1,2,0:T(8,128)}), f32[16,512,16]{1,2,0:T(8,128)S(1)}, u32[]{:S(2)}, u32[]{:S(2)}) async-start(f32[16,512,16]{1,2,0:T(8,128)} %stack.4), calls=%async_computation | async-start | bytes 1048576 | tf_op jit(solution)/shard_map/all_to_all | solution.py:118
  520.7 236.3 %all-reduce.10.cloned.1.call-start = ((), (), s32[]{:S(2)}) async-start(), calls=%async_computation.3 | async-start | bytes 1048576 | tf_op jit(solution)/shard_map/psum | solution.py:20
  1008.4 29.6 %all-to-all-start.1 = ((f32[16,512,16]{1,2,0:T(8,128)}), f32[16,512,16]{1,2,0:T(8,128)S(1)}, u32[]{:S(2)}, u32[]{:S(2)}) async-start(f32[16,512,16]{1,2,0:T(8,128)} %stack.5), calls=%async_computation.1 | async-start | bytes 1048576 | tf_op jit(solution)/shard_map/all_to_all | solution.py:118
  1012.0 240.3 %all-reduce.8.cloned.1.call-start = ((), (), s32[]{:S(2)}) async-start(), calls=%async_computation.2 | async-start | bytes 1048576 | tf_op jit(solution)/shard_map/psum | solution.py:20
  1252.3 8.0 copy-start.4
Sparse Core Ops, SparseCore 0:
  49.7 227.9 all-reduce.11
  548.9 208.0 all-reduce.9
  1044.6 207.7 all-reduce.7
